TPU v7x, 32 devices: a whole 2x2x4 slice. The times are simulated.
32 devices in a mesh: date: 16 (over z, y, core), strip: 2 (over x).
Axes of the slice: x: 2, y: 2, z: 4, core: 2. Of those that a mesh axis runs over, the one named last changes fastest.
Arguments:
- acquisitions: bfloat16 [32, 2, 2, 344, 640], P('date', None, None, None, 'strip'), may hold values from -6 to 6
- shifts: int32 [2, 32, 2, 5, 10], P(None, 'date', None, None, 'strip'), may hold values from -8 to 8, as said below
- fractions: int32 [2, 32, 2, 5, 10], P(None, 'date', None, None, 'strip'), may hold values from 0 to 63
- ref_dates: int32 [2], replicated, may hold values from 0 to 31, as said below
Outputs:
- chip_corr: float32 [2, 32, 2, 5, 10], P(None, 'date', None, None, 'strip')
- coherence: float32 [2, 31, 2, 64, 32], P(None, None, None, 'date', 'strip')
Inputs may be any that keep to these rules, and one draw needn't show every extreme that they name: `shifts`: zero at every chip of date ref_dates[t] in tile t. `ref_dates`: the reference dates of consecutive tiles lie in different blocks of 2 dates.
All inputs are finite; a program needn't handle non-finite values.
Results may differ from a plain program's by a relative error of at most 0.0021.
Values may be sent and summed in bfloat16 or wider, within the bound.
A program may use at most 64 MiB of HBM per device.

v0:
```python
import jax
import jax.numpy as jnp
from jax import lax
from jax.sharding import PartitionSpec as P

TILE_COUNT = 2
CHIP_SIZE = 64
TAP_COUNT = 8
SUBSTEPS = 64
LOOK_AZ = 5
LOOK_RG = 20
MARGIN = 12
epsilon = 1e-06


def padded_2(block, sides, width):
    for axis, dim in sides:
        count = lax.axis_size(axis)
        forward = [(i, i + 1) for i in range(count - 1)]
        backward = [(target, source) for source, target in forward]
        low = lax.ppermute(
            lax.slice_in_dim(block, block.shape[dim] - width, None, axis=dim), axis, forward
        )
        high = lax.ppermute(lax.slice_in_dim(block, 0, width, axis=dim), axis, backward)
        block = jnp.concatenate([low, block, high], axis=dim)
    return block


def spread(value, axis, source):
    kept = jnp.where(lax.axis_index(axis) == source, value, 0).astype(value.dtype)
    return lax.psum(kept, axis)


def passed_along(block, axis, distance):
    devices = range(lax.axis_size(axis))
    route = [(i - distance, i) for i in devices if i - distance in devices]
    return lax.ppermute(block, axis, route)


def sinc_matrix(shift_part, fraction_part):
    window_size = CHIP_SIZE + 2 * MARGIN
    offset = fraction_part.astype(jnp.float32) / SUBSTEPS
    tap_axis = jnp.arange(TAP_COUNT).astype(jnp.float32)
    distance = tap_axis - (TAP_COUNT // 2 - 1) - offset[..., None]
    weights = jnp.sinc(distance) * (0.5 + 0.5 * jnp.cos(jnp.pi * distance / (TAP_COUNT // 2)))
    weights = weights / jnp.sum(weights, axis=-1, keepdims=True)
    out_rows = jnp.arange(CHIP_SIZE, dtype=jnp.int32)[:, None]
    in_rows = jnp.arange(window_size, dtype=jnp.int32)[None, :]
    matrix = jnp.zeros(shift_part.shape + (CHIP_SIZE, window_size), jnp.float32)
    for tap_index in range(TAP_COUNT):
        target = out_rows + shift_part[..., None, None] + (tap_index - TAP_COUNT // 2 + 1 + MARGIN)
        matrix = matrix + jnp.where(
            in_rows == target, weights[..., tap_index][..., None, None], 0.0
        )
    return matrix.astype(jnp.bfloat16)


def correlate(reference_tiles, resampled):
    chips_az = resampled.shape[-2] // CHIP_SIZE
    chips_rg = resampled.shape[-1] // CHIP_SIZE

    def as_chips(values):
        return values.astype(jnp.float32).reshape(
            values.shape[:-2] + (chips_az, CHIP_SIZE, chips_rg, CHIP_SIZE)
        )

    ref_chips = as_chips(reference_tiles)
    sec_chips = as_chips(resampled)
    ref_real = ref_chips[..., 0, :, :, :, :]
    ref_imag = ref_chips[..., 1, :, :, :, :]
    sec_real = sec_chips[..., 0, :, :, :, :]
    sec_imag = sec_chips[..., 1, :, :, :, :]
    cross_real = jnp.sum(ref_real * sec_real + ref_imag * sec_imag, axis=(-3, -1))
    cross_imag = jnp.sum(ref_imag * sec_real - ref_real * sec_imag, axis=(-3, -1))
    ref_power = jnp.sum(ref_real * ref_real + ref_imag * ref_imag, axis=(-3, -1))
    sec_power = jnp.sum(sec_real * sec_real + sec_imag * sec_imag, axis=(-3, -1))
    denominator = jnp.sqrt((ref_power + epsilon) * (sec_power + epsilon))
    return jnp.stack([cross_real / denominator, cross_imag / denominator])


def multilook_pairs(series):
    values = series.astype(jnp.float32)
    earlier = values[:-1]
    second = values[1:]
    early_real = earlier[:, :, 0]
    early_imag = earlier[:, :, 1]
    later_real = second[:, :, 0]
    later_imag = second[:, :, 1]
    cross_real = early_real * later_real + early_imag * later_imag
    cross_imag = early_imag * later_real - early_real * later_imag
    power_early = early_real * early_real + early_imag * early_imag
    power_later = later_real * later_real + later_imag * later_imag

    def box_sum(quantity):
        blocked = quantity.reshape(
            quantity.shape[:2]
            + (quantity.shape[2] // LOOK_AZ, LOOK_AZ, quantity.shape[3] // LOOK_RG, LOOK_RG)
        )
        return jnp.sum(blocked, axis=(3, 5))

    denominator = jnp.sqrt((box_sum(power_early) + epsilon) * (box_sum(power_later) + epsilon))
    return jnp.stack([box_sum(cross_real) / denominator, box_sum(cross_imag) / denominator])


def resample(padded, shift_part, fraction_part):
    window_size = CHIP_SIZE + 2 * MARGIN
    chips_az = shift_part.shape[3]
    chips_rg = shift_part.shape[4]
    pieces = [
        padded[
            :,
            :,
            :,
            chip_row * CHIP_SIZE : chip_row * CHIP_SIZE + window_size,
            chip_col * CHIP_SIZE : chip_col * CHIP_SIZE + window_size,
        ]
        for chip_row in range(chips_az)
        for chip_col in range(chips_rg)
    ]
    windows = jnp.stack(pieces, axis=3).reshape(
        padded.shape[:3] + (chips_az, chips_rg, window_size, window_size)
    )
    azimuth = sinc_matrix(shift_part[0], fraction_part[0])
    across = sinc_matrix(shift_part[1], fraction_part[1])
    partial_rows = jnp.einsum(
        "dtariw,dtcarwv->dtcariv", azimuth, windows, preferred_element_type=jnp.float32
    ).astype(jnp.bfloat16)
    chips_out = jnp.einsum(
        "dtcariv,dtarjv->dtcarij", partial_rows, across, preferred_element_type=jnp.float32
    ).astype(jnp.bfloat16)
    return chips_out.transpose(0, 1, 2, 3, 5, 4, 6).reshape(
        padded.shape[:3] + (chips_az * CHIP_SIZE, chips_rg * CHIP_SIZE)
    )


def per_device(acquisitions, shifts, fractions, ref_dates):
    dates_local = acquisitions.shape[0]
    tile_rows = acquisitions.shape[3] - 2 * MARGIN
    padded = padded_2(acquisitions, (("strip", 4),), MARGIN)
    owners = ref_dates // dates_local
    slots = ref_dates % dates_local
    candidates = [
        lax.dynamic_index_in_dim(acquisitions[:, tile_index], slots[tile_index], 0, keepdims=False)[
            :, MARGIN : MARGIN + tile_rows, :
        ]
        for tile_index in range(TILE_COUNT)
    ]
    reference_tiles = jnp.stack(
        [
            spread(candidates[tile_index], "date", owners[tile_index])
            for tile_index in range(TILE_COUNT)
        ]
    )
    resampled = resample(padded, shifts, fractions)
    chip_corr = correlate(reference_tiles, resampled)
    following = passed_along(resampled[0:1], "date", -1)
    series = jnp.concatenate([resampled, following], axis=0)
    looked = multilook_pairs(series)
    regrouped = lax.all_to_all(looked, "date", split_axis=3, concat_axis=1, tiled=True)
    coherence = regrouped[:, : dates_local * lax.axis_size("date") - 1]
    return (chip_corr, coherence)


def solution(mesh):
    return jax.shard_map(
        per_device,
        mesh=mesh,
        in_specs=(
            P("date", None, None, None, "strip"),
            P(None, "date", None, None, "strip"),
            P(None, "date", None, None, "strip"),
            P(),
        ),
        out_specs=(P(None, "date", None, None, "strip"), P(None, None, None, "date", "strip")),
        check_vma=False,
    )
```

profile of v0, /device:TPU:0, one launch (start us, length us, event | category | flops | bytes accessed | tf_op | source)
XLA Modules:
  0.0 226.9 jit_solution(10947532881645513688)
XLA Ops:
  7.2 1.0 fusion.119
  8.2 1.3 collective-permute-start.1
  9.5 4.9 %collective-permute-start = (bf16[2,2,2,344,12]{3,4,2,1,0:T(8,128)(2,1)S(1)}, bf16[2,2,2,344,12]{3,4,2,1,0:T(8,128)(2,1)S(1)}, u32[]{:S(2)}, u32[]{:S(2)}) collective-permute-start(bf16[2,2,2,344,12]{3,4,2,1,0:T(8,128)(2,1)S(1)} %get-tuple-element.29), channel_id=1, source_target_pairs={{0,1},{2,3},{4,5},{6,7},{8,9},{10,11},{12,13},{14,15},{16,17},{18,... | collective-permute-start | bytes 198152 | tf_op jit(solution)/shard_map/ppermute | solution.py:21
  18.2 1.7 fusion.118
  23.6 1.6 stack.98
  25.2 1.6 stack.97
  26.9 3.2 %fusion.114 = (f32[2,2,5,5]{3,1,2,0:T(2,128)S(1)}, f32[2,2,5,5]{3,1,2,0:T(2,128)S(1)}) fusion(f32[2,2,5,5]{3,1,2,0:T(2,128)S(1)} %get-tuple-element.53, f32[8]{0:T(128)S(1)} %convert_add_fusion, f32[2,2,5,5]{3,1,2,0:T(2,128)S(1)} %get-tuple-element.52), kind=kLoop, calls=%fused_computation.187 | loop fusion | flops 62200 | bytes 1632 | tf_op jit(solution)/shard_map/reduce_sum | solution.py:46
  30.1 3.1 %broadcast_divide_fusion.1 = (f32[2,2,5,5,8]{3,1,2,0,4:T(2,128)S(1)}, f32[2,2,5,5,8]{3,1,2,0,4:T(2,128)S(1)}) fusion(f32[2,2,5,5]{3,1,2,0:T(2,128)S(1)} %get-tuple-element.16, f32[2,2,5,5]{3,1,2,0:T(2,128)S(1)} %get-tuple-element.53, f32[8]{0:T(128)S(1)} %convert_add_fusion, f32[2,2,5,5]{3,1,2,0:T(2,128)S(1)} %get-tuple-element.17, ...), kind=kLoop, calls=%fused_computation.185 | loop fusion | flops 62400 | bytes 8032 | tf_op jit(solution)/shard_map/div | solution.py:46
  33.2 0.9 fusion.104
  42.3 0.8 fusion.70
  43.2 0.8 bitcast_dynamic-update-slice_fusion.11
  44.0 0.8 bitcast_dynamic-update-slice_fusion.10
  44.8 0.8 bitcast_dynamic-update-slice_fusion.9
  45.7 0.8 fusion.69
  50.1 0.9 fusion.66
  51.0 0.8 bitcast_dynamic-update-slice_fusion.5
  51.8 0.8 bitcast_dynamic-update-slice_fusion.4
  52.7 0.8 bitcast_dynamic-update-slice_fusion.3
  53.5 0.8 fusion.65
  58.0 7.2 %copy.165 = bf16[2,2,2,25,88,88]{5,4,2,3,1,0:T(8,128)(2,1)} copy(bf16[2,2,2,25,88,88]{4,5,2,1,0,3:T(8,128)(2,1)} %fusion.62) | data formatting | bytes 6195200 | tf_op jit(solution)/shard_map/stack | solution.py:120
  65.4 13.2 %fusion.4.clone.5 = bf16[2,2,2,5,5,64,88]{6,5,2,4,3,1,0:T(8,128)(2,1)S(1)} fusion(bf16[2,2,2,5,5,88,88]{6,5,2,4,3,1,0:T(8,128)(2,1)} %bitcast.221, f32[2,2,5,5]{3,2,1,0:T(8,128)S(1)} %copy.174, s32[2,2,5,5,64]{4,3,2,1,0:T(8,128)S(1)} %get-tuple-element.63, f32[2,2,5,5]{3,2,1,0:T(8,128)S(1)} %copy.173, ...), kind=kOutput, calls=%fused_computation.3.clone.clone.clone.clone.clone.2 | convolution fusion | flops 212889600 | bytes 5558400 | tf_op jit(solution)/shard_map/dtariw,dtcarwv->dtcariv/dot_general | solution.py:125
  78.7 13.6 %fusion.122 = (f32[2,2,2,5,64,5,64]{4,6,2,5,3,1,0:T(8,128)}, bf16[2,2,2,5,64,5,64]{4,6,2,5,3,1,0:T(8,128)(2,1)S(1)}) fusion(f32[2,2,5,5]{3,2,1,0:T(8,128)S(1)} %copy-done.13, s32[2,2,5,5,64]{4,3,2,1,0:T(8,128)S(1)} %copy-done.5, f32[2,2,5,5]{3,2,1,0:T(8,128)S(1)} %copy-done.12, s32[2,2,5,5,64]{4,3,2,1,0:T(8,128)S(1)} %copy-done.4, ...), kind=kOutput, calls=%fused_computation.226 | convolution fusion | flops 159334400 | bytes 7376000 | tf_op jit(solution)/shard_map/dtcariv,dtarjv->dtcarij/dot_general | solution.py:128
  92.3 1.4 slice.307
  93.7 5.2 %copy.181 = bf16[2,2,2,5,64,5,64]{6,5,4,3,2,1,0:T(8,128)(2,1)} copy(bf16[2,2,2,5,64,5,64]{4,6,2,5,3,1,0:T(8,128)(2,1)S(1)} %get-tuple-element.79) | data formatting | bytes 3276800 | tf_op jit(solution)/shard_map/convert_element_type | solution.py:130
  98.9 3.2 %copy.182 = bf16[1,2,2,5,64,5,64]{6,5,4,3,2,1,0:T(8,128)(2,1)S(1)} copy(bf16[1,2,2,5,64,5,64]{4,6,2,5,3,1,0:T(8,128)(2,1)} %slice.307) | data formatting | bytes 1638400 | tf_op jit(solution)/shard_map/slice | solution.py:156
  102.2 2.2 slice.274
  104.3 1.5 collective-permute-start.2
  105.8 7.2 %reshape.241 = bf16[2,2,2,320,320]{4,3,2,1,0:T(8,128)(2,1)} reshape(bf16[2,2,2,5,64,5,64]{6,5,4,3,2,1,0:T(8,128)(2,1)} %copy.181) | data formatting | bytes 3276800 | tf_op jit(solution)/shard_map/reshape | solution.py:131
  113.0 19.2 %all-reduce.3.cloned.1.call-done = (bf16[1,2,5,64,5,64]{5,4,3,2,1,0:T(8,128)(2,1)}, bf16[1,2,5,64,5,64]{5,4,3,2,1,0:T(8,128)(2,1)}) async-done(((bf16[1,2,5,64,5,64]{5,4,3,2,1,0:T(8,128)(2,1)}, bf16[1,2,5,64,5,64]{5,4,3,2,1,0:T(8,128)(2,1)}), (bf16[1,2,5,64,5,64]{5,4,3,2,1,0:T(8,128)(2,1)}, bf16[1,2,5,64,5,64]{5,4,3,2,1,0:T(8,128)(2,1)})) %all-reduce.3.cloned.1.call-update) | async-done | bytes 819216 | tf_op jit(solution)/shard_map/psum | solution.py:31
  132.2 2.7 %maximum_convert_fusion.1 = f32[2,2,5,64,5,64]{5,4,3,2,1,0:T(8,128)S(1)} fusion(bf16[1,2,5,64,5,64]{5,4,3,2,1,0:T(8,128)(2,1)} %get-tuple-element.18, bf16[1,2,5,64,5,64]{5,4,3,2,1,0:T(8,128)(2,1)} %get-tuple-element.19), kind=kLoop, calls=%fused_computation.30 | loop fusion | flops 819200 | bytes 2457600 | tf_op jit(solution)/shard_map/convert_element_type | solution.py:63
  135.5 2.0 slice_bitcast_fusion.3
  137.5 2.9 %copy.155 = f32[2,5,64,5,64]{2,4,3,1,0:T(8,128)} copy(f32[2,5,64,5,64]{4,3,2,1,0:T(8,128)} %get-tuple-element.24) | data formatting | bytes 1638400 | tf_op jit(solution)/shard_map/mul | solution.py:73
  140.4 1.7 copy.176
  142.0 5.0 %add_reduce_fusion.1 = (f32[2,2,5,5]{3,2,1,0:T(8,128)S(1)}, f32[2,2,5,5]{3,2,1,0:T(8,128)S(1)}, f32[2,2,5,5]{3,2,1,0:T(8,128)S(1)}) fusion(f32[2,2,2,5,64,5,64]{4,6,2,5,3,1,0:T(8,128)} %get-tuple-element.78, f32[2,5,64,5,64]{2,4,3,1,0:T(8,128)} %copy.176, f32[2,5,64,5,64]{2,4,3,1,0:T(8,128)} %copy.155), kind=kLoop, calls=%fused_computation.6 | loop fusion | flops 4914900 | bytes 4916400 | tf_op jit(solution)/shard_map/reduce_sum | solution.py:73
  147.1 1.8 maximum_convert_fusion
  148.9 2.8 %multiply_add_fusion.2 = (f32[2,2,1,320,320]{4,3,2,1,0:T(8,128)}, f32[2,2,1,320,320]{4,3,2,1,0:T(8,128)}, f32[2,2,1,320,320]{4,3,2,1,0:T(8,128)}, f32[2,2,1,320,320]{4,3,2,1,0:T(8,128)S(1)}) fusion(f32[3,2,2,320,320]{4,3,2,1,0:T(8,128)S(1)} %maximum_convert_fusion), kind=kLoop, calls=%fused_computation.35 | loop fusion | flops 4915200 | bytes 13107200 | tf_op jit(solution)/shard_map/add | solution.py:89
  151.7 9.1 %add.572 = f32[2,2,64,5,16,20]{5,4,3,2,1,0:T(8,128)} reshape(f32[2,2,1,320,320]{4,3,2,1,0:T(8,128)} %get-tuple-element.20) | data formatting | bytes 3276800 | tf_op jit(solution)/shard_map/add | solution.py:89
  160.8 9.0 %add.574 = f32[2,2,64,5,16,20]{5,4,3,2,1,0:T(8,128)} reshape(f32[2,2,1,320,320]{4,3,2,1,0:T(8,128)} %get-tuple-element.21) | data formatting | bytes 3276800 | tf_op jit(solution)/shard_map/add | solution.py:91
  169.8 4.8 %reduce_sum.102 = f32[2,2,64,16]{3,2,1,0:T(8,128)S(1)} reduce(f32[2,2,64,5,16,20]{5,4,3,2,1,0:T(8,128)} %add.572, f32[]{:T(128)} %constant.98.clone.1), dimensions={3,5}, to_apply=%region_8.10 | reduce | flops 405504 | bytes 1654788 | tf_op jit(solution)/shard_map/reduce_sum | solution.py:99
  174.6 4.8 %reduce_sum.103 = f32[2,2,64,16]{3,2,1,0:T(8,128)S(1)} reduce(f32[2,2,64,5,16,20]{5,4,3,2,1,0:T(8,128)} %add.574, f32[]{:T(128)} %constant.98.clone.1), dimensions={3,5}, to_apply=%region_9.11 | reduce | flops 405504 | bytes 1654788 | tf_op jit(solution)/shard_map/reduce_sum | solution.py:99
  179.4 9.1 %add.577 = f32[2,2,64,5,16,20]{5,4,3,2,1,0:T(8,128)} reshape(f32[2,2,1,320,320]{4,3,2,1,0:T(8,128)} %get-tuple-element.22) | data formatting | bytes 3276800 | tf_op jit(solution)/shard_map/add | solution.py:92
  188.5 4.8 %reduce_sum.104 = f32[2,2,64,16]{3,2,1,0:T(8,128)S(1)} reduce(f32[2,2,64,5,16,20]{5,4,3,2,1,0:T(8,128)} %add.577, f32[]{:T(128)} %constant.98.clone.1), dimensions={3,5}, to_apply=%region_10.12 | reduce | flops 405504 | bytes 1654788 | tf_op jit(solution)/shard_map/reduce_sum | solution.py:99
  193.3 7.9 %sub.65 = f32[2,2,64,5,16,20]{5,4,3,2,1,0:T(8,128)} reshape(f32[2,2,1,320,320]{4,3,2,1,0:T(8,128)S(1)} %get-tuple-element.23) | data formatting | bytes 3276800 | tf_op jit(solution)/shard_map/sub | solution.py:90
  201.2 4.8 %reduce_sum.105 = f32[2,2,64,16]{3,2,1,0:T(8,128)S(1)} reduce(f32[2,2,64,5,16,20]{5,4,3,2,1,0:T(8,128)} %sub.65, f32[]{:T(128)} %constant.98.clone.1), dimensions={3,5}, to_apply=%region_11.13 | reduce | flops 405504 | bytes 1654788 | tf_op jit(solution)/shard_map/reduce_sum | solution.py:99
  206.3 0.9 reshape.244
  207.3 3.5 %all-to-all-start = ((f32[16,1,512]{2,1,0:T(1,128)}), f32[16,1,512]{2,1,0:T(1,128)S(1)}, u32[]{:S(2)}, u32[]{:S(2)}) async-start(f32[16,1,512]{2,1,0:T(1,128)} %reshape.244), calls=%async_computation | async-start | bytes 65536 | tf_op jit(solution)/shard_map/all_to_all | solution.py:159
  211.4 6.0 %all-to-all-done = f32[16,1,512]{2,1,0:T(1,128)S(1)} async-done(((f32[16,1,512]{2,1,0:T(1,128)}), f32[16,1,512]{2,1,0:T(1,128)S(1)}, u32[]{:S(2)}, u32[]{:S(2)}) %all-to-all-start) | async-done | bytes 32800 | tf_op jit(solution)/shard_map/all_to_all | solution.py:159
  219.3 0.8 copy.186
  (98 shorter events, 21.4 us)
Async XLA Ops:
  7.2 125.0 %all-reduce.3.cloned.1.call-start = ((), (), s32[]{:S(2)}) async-start(), calls=%async_computation.1 | async-start | bytes 5242880 | tf_op jit(solution)/shard_map/psum | solution.py:31
  8.2 33.4 %collective-permute-start.1 = (bf16[2,2,2,344,12]{3,4,2,1,0:T(8,128)(2,1)S(1)}, bf16[2,2,2,344,12]{3,4,2,1,0:T(8,128)(2,1)S(1)}, u32[]{:S(2)}, u32[]{:S(2)}) collective-permute-start(bf16[2,2,2,344,12]{3,4,2,1,0:T(8,128)(2,1)S(1)} %get-tuple-element.28), channel_id=1, source_target_pairs={{1,0},{3,2},{5,4},{7,6},{9,8},{11,10},{13,12},{15,14},{17,16},{19,... | collective-permute-start | bytes 198152 | tf_op jit(solution)/shard_map/ppermute | solution.py:24
  9.5 29.1 %collective-permute-start = (bf16[2,2,2,344,12]{3,4,2,1,0:T(8,128)(2,1)S(1)}, bf16[2,2,2,344,12]{3,4,2,1,0:T(8,128)(2,1)S(1)}, u32[]{:S(2)}, u32[]{:S(2)}) collective-permute-start(bf16[2,2,2,344,12]{3,4,2,1,0:T(8,128)(2,1)S(1)} %get-tuple-element.29), channel_id=1, source_target_pairs={{0,1},{2,3},{4,5},{6,7},{8,9},{10,11},{12,13},{14,15},{16,17},{18,... | collective-permute-start | bytes 198152 | tf_op jit(solution)/shard_map/ppermute | solution.py:21
  23.6 3.2 %copy-start.7 = (s32[2,2,2,5,5]{4,2,3,1,0:T(2,128)S(1)}, s32[2,2,2,5,5]{4,2,3,1,0:T(2,128)}, u32[]{:S(2)}) copy-start(s32[2,2,2,5,5]{4,2,3,1,0:T(2,128)} %param.6) | copy-start | bytes 2404
  23.6 3.3 %copy-start.8 = (s32[2,2,2,5,5]{4,2,3,1,0:T(2,128)S(1)}, s32[2,2,2,5,5]{4,2,3,1,0:T(2,128)}, u32[]{:S(2)}) copy-start(s32[2,2,2,5,5]{4,2,3,1,0:T(2,128)} %param.7) | copy-start | bytes 2404
  25.2 8.9 %copy-start = (bf16[2,2,2,344,320]{3,4,2,1,0:T(8,128)(2,1)S(1)}, bf16[2,2,2,344,320]{3,4,2,1,0:T(8,128)(2,1)}, u32[]{:S(2)}) copy-start(bf16[2,2,2,344,320]{3,4,2,1,0:T(8,128)(2,1)} %param.5) | copy-start | bytes 5283844
  58.0 7.3 %copy-start.15 = (f32[2,2,5,5]{3,2,1,0:T(8,128)S(1)}, f32[2,2,5,5]{3,2,1,0:T(8,128)}, u32[]{:S(2)}) copy-start(f32[2,2,5,5]{3,2,1,0:T(8,128)} %copy.168) | copy-start | bytes 1204
  65.3 13.3 %copy-start.2 = (s32[2,2,5,5,64]{4,3,2,1,0:T(8,128)S(1)}, s32[2,2,5,5,64]{4,3,2,1,0:T(8,128)}, u32[]{:S(2)}) copy-start(s32[2,2,5,5,64]{4,3,2,1,0:T(8,128)} %get-tuple-element.93) | copy-start | bytes 76804
  65.3 13.3 %copy-start.3 = (s32[2,2,5,5,64]{4,3,2,1,0:T(8,128)S(1)}, s32[2,2,5,5,64]{4,3,2,1,0:T(8,128)}, u32[]{:S(2)}) copy-start(s32[2,2,5,5,64]{4,3,2,1,0:T(8,128)} %get-tuple-element.94) | copy-start | bytes 76804
  65.3 13.3 %copy-start.4 = (s32[2,2,5,5,64]{4,3,2,1,0:T(8,128)S(1)}, s32[2,2,5,5,64]{4,3,2,1,0:T(8,128)}, u32[]{:S(2)}) copy-start(s32[2,2,5,5,64]{4,3,2,1,0:T(8,128)} %get-tuple-element.95) | copy-start | bytes 76804
  65.3 13.3 %copy-start.5 = (s32[2,2,5,5,64]{4,3,2,1,0:T(8,128)S(1)}, s32[2,2,5,5,64]{4,3,2,1,0:T(8,128)}, u32[]{:S(2)}) copy-start(s32[2,2,5,5,64]{4,3,2,1,0:T(8,128)} %get-tuple-element.96) | copy-start | bytes 76804
  65.3 13.3 %copy-start.6 = (s32[2,2,5,5,64]{4,3,2,1,0:T(8,128)S(1)}, s32[2,2,5,5,64]{4,3,2,1,0:T(8,128)}, u32[]{:S(2)}) copy-start(s32[2,2,5,5,64]{4,3,2,1,0:T(8,128)} %get-tuple-element.97) | copy-start | bytes 76804
  65.3 13.3 %copy-start.9 = (f32[2,2,5,5]{3,2,1,0:T(8,128)S(1)}, f32[2,2,5,5]{3,2,1,0:T(8,128)}, u32[]{:S(2)}) copy-start(f32[2,2,5,5]{3,2,1,0:T(8,128)} %copy.160) | copy-start | bytes 1204
  65.3 13.3 %copy-start.10 = (f32[2,2,5,5]{3,2,1,0:T(8,128)S(1)}, f32[2,2,5,5]{3,2,1,0:T(8,128)}, u32[]{:S(2)}) copy-start(f32[2,2,5,5]{3,2,1,0:T(8,128)} %copy.161) | copy-start | bytes 1204
  65.3 13.3 %copy-start.11 = (f32[2,2,5,5]{3,2,1,0:T(8,128)S(1)}, f32[2,2,5,5]{3,2,1,0:T(8,128)}, u32[]{:S(2)}) copy-start(f32[2,2,5,5]{3,2,1,0:T(8,128)} %copy.162) | copy-start | bytes 1204
  65.3 13.3 %copy-start.12 = (f32[2,2,5,5]{3,2,1,0:T(8,128)S(1)}, f32[2,2,5,5]{3,2,1,0:T(8,128)}, u32[]{:S(2)}) copy-start(f32[2,2,5,5]{3,2,1,0:T(8,128)} %copy.163) | copy-start | bytes 1204
  65.3 13.3 %copy-start.13 = (f32[2,2,5,5]{3,2,1,0:T(8,128)S(1)}, f32[2,2,5,5]{3,2,1,0:T(8,128)}, u32[]{:S(2)}) copy-start(f32[2,2,5,5]{3,2,1,0:T(8,128)} %copy.164) | copy-start | bytes 1204
  65.3 13.3 %copy-start.14 = (f32[2,2,5,5]{3,2,1,0:T(8,128)S(1)}, f32[2,2,5,5]{3,2,1,0:T(8,128)}, u32[]{:S(2)}) copy-start(f32[2,2,5,5]{3,2,1,0:T(8,128)} %copy.157) | copy-start | bytes 1204
  104.3 42.8 %collective-permute-start.2 = (bf16[1,2,2,320,320]{4,3,2,1,0:T(8,128)(2,1)}, bf16[1,2,2,320,320]{4,3,2,1,0:T(8,128)(2,1)}, u32[]{:S(2)}, u32[]{:S(2)}) collective-permute-start(bf16[1,2,2,320,320]{4,3,2,1,0:T(8,128)(2,1)} %slice.274), channel_id=1, source_target_pairs={{2,0},{4,2},{6,4},{8,6},{10,8},{12,10},{14,12},{16,14},{18,16},{20... | collective-permute-start | bytes 2457608 | tf_op jit(solution)/shard_map/ppermute | solution.py:37
  142.0 5.1 %copy-start.1 = (bf16[2,2,2,320,320]{4,3,2,1,0:T(8,128)(2,1)S(1)}, bf16[2,2,2,320,320]{4,3,2,1,0:T(8,128)(2,1)}, u32[]{:S(2)}) copy-start(bf16[2,2,2,320,320]{4,3,2,1,0:T(8,128)(2,1)} %reshape.241) | copy-start | bytes 4915204
  207.3 10.1 %all-to-all-start = ((f32[16,1,512]{2,1,0:T(1,128)}), f32[16,1,512]{2,1,0:T(1,128)S(1)}, u32[]{:S(2)}, u32[]{:S(2)}) async-start(f32[16,1,512]{2,1,0:T(1,128)} %reshape.244), calls=%async_computation | async-start | bytes 65536 | tf_op jit(solution)/shard_map/all_to_all | solution.py:159
Sparse Core Ops, SparseCore 0:
  26.9 105.2 all-reduce.2
where the time goes:
time: 228 us; the launch traced here: 227 us
  local copies, waits for them, and re-layouts  98.4 us (43%)
  other arithmetic  45.7 us (20%)
  matrix products  26.8 us (12%)
  waiting for transfers between devices  25.2 us (11%)
  between operations  19.6 us (9%)
  starting transfers between devices  11.2 us (5%)
    psum x1, waiting for transfers between devices, spread(): return lax.psum(kept, axis)  19.2 us
    reduce_sum x4, other arithmetic, box_sum(): return jnp.sum(blocked, axis=(3, 5))  19.2 us
    unnamed x55, local copies, waits for them, and re-layouts  17.1 us
    dot_general x1, matrix products, resample(): jnp.einsum('dtcariv,dtarjv->dtcarij', partial_rows, across, preferred_ele...  13.6 us
    dot_general x1, matrix products, resample(): jnp.einsum('dtariw,dtcarwv->dtcariv', azimuth, windows, preferred_element...  13.2 us
    add x1, local copies, waits for them, and re-layouts, multilook_pairs(): power_later = later_real * later_real + later_imag * later_imag  9.09 us
    add x1, local copies, waits for them, and re-layouts, multilook_pairs(): cross_real = early_real * later_real + early_imag * later_imag  9.08 us
    add x1, local copies, waits for them, and re-layouts, multilook_pairs(): power_early = early_real * early_real + early_imag * early_imag  9.02 us
  transfers between devices with their start and end apart: 5, of which 2 were waited for; matrix products, arithmetic and copies ran while one was open for 47% of the time, Pallas kernels for 0%

commit v1 on v0

--- a/solution.py
+++ b/solution.py
@@ -28,7 +28,7 @@
 
 def spread(value, axis, source):
     kept = jnp.where(lax.axis_index(axis) == source, value, 0).astype(value.dtype)
-    return lax.psum(kept, axis)
+    return jnp.sum(lax.all_gather(kept, axis), axis=0)
 
 
 def passed_along(block, axis, distance):

time: 228 us -> 236 us (1.035)
  blocking collectives: 0 us -> 28.5 us
  waiting for transfers between devices: 25.2 us -> 0.06 us
  other arithmetic: 45.7 us -> 54.1 us
  starting transfers between devices: 11.2 us -> 7.72 us
    all_to_all x0 -> x1, blocking collectives: none -> 28.5 us  [per_device(): lax.all_to_all(looked, 'date', split_axis=3, concat_axis=1, tiled=True)]
    psum x1 -> x0, waiting for transfers between devices: 19.2 us -> none  [spread(): return lax.psum(kept, axis)]
    reduce_sum x0 -> x2, other arithmetic: none -> 9.32 us  [spread(): return jnp.sum(lax.all_gather(kept, axis), axis=0)]
    all_to_all x1 -> x0, waiting for transfers between devices: 5.98 us -> none  [per_device(): lax.all_to_all(looked, 'date', split_axis=3, concat_axis=1, tiled=True)]
    broadcast_in_dim x17, local copies, waits for them, and re-layouts: 4.27 us -> 0.08 us  [sinc_matrix(): jnp.where(in_rows == target, weights[..., tap_index][..., None, None], 0.0)]
    dynamic_slice x0 -> x4, local copies, waits for them, and re-layouts: none -> 3.69 us  [per_device(): lax.dynamic_index_in_dim(acquisitions[:, tile_index], slots[tile_index],...]
    all_to_all x1 -> x0, starting transfers between devices: 3.5 us -> none  [per_device(): lax.all_to_all(looked, 'date', split_axis=3, concat_axis=1, tiled=True)]
    convert_element_type x1, local copies, waits for them, and re-layouts: 5.24 us -> 7.72 us  [resample(): chips_out = jnp.einsum('dtcariv,dtarjv->dtcarij', partial_rows, across, p...]
  transfers between devices with their start and end apart: 5 -> 5, of which waited for: 2 -> 0; matrix products, arithmetic and copies ran while one was open for 47% -> 63% of each run, Pallas kernels for 0% -> 0%
where the time goes in v1:
time: 236 us; the launch traced here: 235 us
  local copies, waits for them, and re-layouts  98 us (42%)
  other arithmetic  54.1 us (23%)
  blocking collectives  28.5 us (12%)
  matrix products  26.6 us (11%)
  between operations  19.8 us (8%)
  starting transfers between devices  7.72 us (3%)
    all_to_all x1, blocking collectives, per_device(): lax.all_to_all(looked, 'date', split_axis=3, concat_axis=1, tiled=True)  28.5 us
    reduce_sum x4, other arithmetic, box_sum(): return jnp.sum(blocked, axis=(3, 5))  19.8 us
    unnamed x31, local copies, waits for them, and re-layouts  18 us
    dot_general x1, matrix products, resample(): jnp.einsum('dtcariv,dtarjv->dtcarij', partial_rows, across, preferred_ele...  13.6 us
    dot_general x1, matrix products, resample(): jnp.einsum('dtariw,dtcarwv->dtcariv', azimuth, windows, preferred_element...  13 us
    reduce_sum x2, other arithmetic, spread(): return jnp.sum(lax.all_gather(kept, axis), axis=0)  9.32 us
    add x1, local copies, waits for them, and re-layouts, multilook_pairs(): power_later = later_real * later_real + later_imag * later_imag  9.12 us
    add x1, local copies, waits for them, and re-layouts, multilook_pairs(): cross_real = early_real * later_real + early_imag * later_imag  9.12 us
  transfers between devices with their start and end apart: 5, of which 0 were waited for; matrix products, arithmetic and copies ran while one was open for 63% of the time, Pallas kernels for 0%

profile of v1, /device:TPU:0, one launch (start us, length us, event | category | flops | bytes accessed | tf_op | source)
XLA Modules:
  0.0 234.8 jit_solution(14353365737267427088)
XLA Ops:
  9.9 2.7 %fusion.118 = (bf16[2,1,2,344,320]{3,4,2,1,0:T(8,128)(2,1)}, bf16[2,1,2,344,320]{3,4,2,1,0:T(8,128)(2,1)S(1)}) fusion(bf16[2,2,2,344,320]{3,4,2,1,0:T(8,128)(2,1)} %param.5), kind=kLoop, calls=%fused_computation.222 | loop fusion | bytes 3522560 | tf_op jit(solution)/shard_map/slice | solution.py:143
  13.2 2.0 constant_dynamic-slice_fusion.1
  15.3 1.3 copy.131
  17.3 1.0 slice_select_fusion.1
  21.2 1.0 slice_select_fusion
  22.2 1.3 collective-permute-start.1
  23.5 4.9 %collective-permute-start = (bf16[2,2,2,344,12]{3,4,2,1,0:T(8,128)(2,1)S(1)}, bf16[2,2,2,344,12]{3,4,2,1,0:T(8,128)(2,1)S(1)}, u32[]{:S(2)}, u32[]{:S(2)}) collective-permute-start(bf16[2,2,2,344,12]{3,4,2,1,0:T(8,128)(2,1)S(1)} %get-tuple-element.25), channel_id=1, source_target_pairs={{0,1},{2,3},{4,5},{6,7},{8,9},{10,11},{12,13},{14,15},{16,17},{18,... | collective-permute-start | bytes 198152 | tf_op jit(solution)/shard_map/ppermute | solution.py:21
  28.5 3.2 %fusion.114 = (f32[2,2,5,5]{3,1,2,0:T(2,128)S(1)}, f32[2,2,5,5]{3,1,2,0:T(2,128)S(1)}) fusion(f32[2,2,5,5]{3,1,2,0:T(2,128)S(1)} %get-tuple-element.49, f32[8]{0:T(128)S(1)} %convert_add_fusion, f32[2,2,5,5]{3,1,2,0:T(2,128)S(1)} %get-tuple-element.48), kind=kLoop, calls=%fused_computation.185 | loop fusion | flops 62200 | bytes 1632 | tf_op jit(solution)/shard_map/reduce_sum | solution.py:46
  31.7 3.1 %broadcast_divide_fusion.1 = (f32[2,2,5,5,8]{3,1,2,0,4:T(2,128)S(1)}, f32[2,2,5,5,8]{3,1,2,0,4:T(2,128)S(1)}) fusion(f32[2,2,5,5]{3,1,2,0:T(2,128)S(1)} %get-tuple-element.14, f32[2,2,5,5]{3,1,2,0:T(2,128)S(1)} %get-tuple-element.49, f32[8]{0:T(128)S(1)} %convert_add_fusion, f32[2,2,5,5]{3,1,2,0:T(2,128)S(1)} %get-tuple-element.15, ...), kind=kLoop, calls=%fused_computation.183 | loop fusion | flops 62400 | bytes 8032 | tf_op jit(solution)/shard_map/div | solution.py:46
  39.2 0.8 fusion.70
  40.0 0.8 bitcast_dynamic-update-slice_fusion.11
  40.9 0.8 bitcast_dynamic-update-slice_fusion.10
  41.7 0.8 bitcast_dynamic-update-slice_fusion.9
  42.5 0.8 fusion.69
  46.9 0.9 fusion.66
  47.8 0.8 bitcast_dynamic-update-slice_fusion.5
  48.6 0.8 bitcast_dynamic-update-slice_fusion.4
  49.5 0.8 bitcast_dynamic-update-slice_fusion.3
  50.3 0.8 fusion.65
  52.6 0.7 bitcast_dynamic-update-slice_fusion.1
  54.7 7.2 %copy.148 = bf16[2,2,2,25,88,88]{5,4,2,3,1,0:T(8,128)(2,1)} copy(bf16[2,2,2,25,88,88]{4,5,2,1,0,3:T(8,128)(2,1)} %fusion.62) | data formatting | bytes 6195200 | tf_op jit(solution)/shard_map/stack | solution.py:120
  61.9 13.0 %fusion.4.clone.5 = bf16[2,2,2,5,5,64,88]{6,5,2,4,3,1,0:T(8,128)(2,1)S(1)} fusion(bf16[2,2,2,5,5,88,88]{6,5,2,4,3,1,0:T(8,128)(2,1)} %bitcast.223, f32[2,2,5,5]{3,2,1,0:T(8,128)S(1)} %copy.157, s32[2,2,5,5,64]{4,3,2,1,0:T(8,128)S(1)} %get-tuple-element.59, f32[2,2,5,5]{3,2,1,0:T(8,128)S(1)} %copy.156, ...), kind=kOutput, calls=%fused_computation.3.clone.clone.clone.clone.clone.2 | convolution fusion | flops 212889600 | bytes 5558400 | tf_op jit(solution)/shard_map/dtariw,dtcarwv->dtcariv/dot_general | solution.py:125
  75.0 13.6 %fusion.122 = (f32[2,2,2,5,64,5,64]{4,6,2,5,3,1,0:T(8,128)}, bf16[2,2,2,5,64,5,64]{4,6,2,5,3,1,0:T(8,128)(2,1)S(1)}) fusion(f32[2,2,5,5]{3,2,1,0:T(8,128)S(1)} %copy.147, s32[2,2,5,5,64]{4,3,2,1,0:T(8,128)S(1)} %get-tuple-element.92, f32[2,2,5,5]{3,2,1,0:T(8,128)S(1)} %copy.146, s32[2,2,5,5,64]{4,3,2,1,0:T(8,128)S(1)} %get-tuple-element.91, ...), kind=kOutput, calls=%fused_computation.226 | convolution fusion | flops 159334400 | bytes 7376000 | tf_op jit(solution)/shard_map/dtcariv,dtarjv->dtcarij/dot_general | solution.py:128
  88.5 1.7 copy-done.1
  90.4 2.8 %copy.165 = bf16[1,2,2,5,64,5,64]{6,5,4,3,2,1,0:T(8,128)(2,1)} copy(bf16[1,2,2,5,64,5,64]{4,6,2,5,3,1,0:T(8,128)(2,1)S(1)} %slice.307) | data formatting | bytes 1638400 | tf_op jit(solution)/shard_map/slice | solution.py:156
  93.2 3.3 %slice.274 = bf16[1,2,2,320,320]{4,3,2,1,0:T(8,128)(2,1)S(1)} reshape(bf16[1,2,2,5,64,5,64]{6,5,4,3,2,1,0:T(8,128)(2,1)} %copy.165) | data formatting | bytes 1638400 | tf_op jit(solution)/shard_map/slice | solution.py:156
  96.5 1.5 collective-permute-start.2
  98.0 7.7 %copy.164 = bf16[2,2,2,5,64,5,64]{6,5,4,3,2,1,0:T(8,128)(2,1)} copy(bf16[2,2,2,5,64,5,64]{4,6,2,5,3,1,0:T(8,128)(2,1)} %copy-done.1) | data formatting | bytes 3276800 | tf_op jit(solution)/shard_map/convert_element_type | solution.py:130
  105.7 6.1 %reshape.241 = bf16[2,2,2,320,320]{4,3,2,1,0:T(8,128)(2,1)S(1)} reshape(bf16[2,2,2,5,64,5,64]{6,5,4,3,2,1,0:T(8,128)(2,1)} %copy.164) | data formatting | bytes 3276800 | tf_op jit(solution)/shard_map/reshape | solution.py:131
  111.8 1.8 maximum_convert_fusion
  113.6 2.9 %multiply_add_fusion.2 = (f32[2,2,1,320,320]{4,3,2,1,0:T(8,128)}, f32[2,2,1,320,320]{4,3,2,1,0:T(8,128)}, f32[2,2,1,320,320]{4,3,2,1,0:T(8,128)}, f32[2,2,1,320,320]{4,3,2,1,0:T(8,128)S(1)}) fusion(f32[3,2,2,320,320]{4,3,2,1,0:T(8,128)S(1)} %maximum_convert_fusion), kind=kLoop, calls=%fused_computation.35 | loop fusion | flops 4915200 | bytes 13107200 | tf_op jit(solution)/shard_map/add | solution.py:89
  116.4 9.1 %add.568 = f32[2,2,64,5,16,20]{5,4,3,2,1,0:T(8,128)} reshape(f32[2,2,1,320,320]{4,3,2,1,0:T(8,128)} %get-tuple-element.16) | data formatting | bytes 3276800 | tf_op jit(solution)/shard_map/add | solution.py:89
  125.5 9.0 %add.570 = f32[2,2,64,5,16,20]{5,4,3,2,1,0:T(8,128)} reshape(f32[2,2,1,320,320]{4,3,2,1,0:T(8,128)} %get-tuple-element.17) | data formatting | bytes 3276800 | tf_op jit(solution)/shard_map/add | solution.py:91
  134.6 4.8 %reduce_sum.128 = f32[2,2,64,16]{3,2,1,0:T(8,128)S(1)} reduce(f32[2,2,64,5,16,20]{5,4,3,2,1,0:T(8,128)} %add.568, f32[]{:T(128)} %constant.100.clone.1), dimensions={3,5}, to_apply=%region_8.10 | reduce | flops 405504 | bytes 1654788 | tf_op jit(solution)/shard_map/reduce_sum | solution.py:99
  139.4 4.9 %reduce_sum.129 = f32[2,2,64,16]{3,2,1,0:T(8,128)S(1)} reduce(f32[2,2,64,5,16,20]{5,4,3,2,1,0:T(8,128)} %add.570, f32[]{:T(128)} %constant.100.clone.1), dimensions={3,5}, to_apply=%region_9.11 | reduce | flops 405504 | bytes 1654788 | tf_op jit(solution)/shard_map/reduce_sum | solution.py:99
  144.3 9.1 %add.573 = f32[2,2,64,5,16,20]{5,4,3,2,1,0:T(8,128)} reshape(f32[2,2,1,320,320]{4,3,2,1,0:T(8,128)} %get-tuple-element.18) | data formatting | bytes 3276800 | tf_op jit(solution)/shard_map/add | solution.py:92
  153.4 5.0 %reduce_sum.130 = f32[2,2,64,16]{3,2,1,0:T(8,128)S(1)} reduce(f32[2,2,64,5,16,20]{5,4,3,2,1,0:T(8,128)} %add.573, f32[]{:T(128)} %constant.100.clone.1), dimensions={3,5}, to_apply=%region_10.12 | reduce | flops 405504 | bytes 1654788 | tf_op jit(solution)/shard_map/reduce_sum | solution.py:99
  158.4 8.0 %sub.65 = f32[2,2,64,5,16,20]{5,4,3,2,1,0:T(8,128)} reshape(f32[2,2,1,320,320]{4,3,2,1,0:T(8,128)S(1)} %get-tuple-element.19) | data formatting | bytes 3276800 | tf_op jit(solution)/shard_map/sub | solution.py:90
  166.4 5.0 %reduce_sum.131 = f32[2,2,64,16]{3,2,1,0:T(8,128)S(1)} reduce(f32[2,2,64,5,16,20]{5,4,3,2,1,0:T(8,128)} %sub.65, f32[]{:T(128)} %constant.100.clone.1), dimensions={3,5}, to_apply=%region_11.13 | reduce | flops 405504 | bytes 1654788 | tf_op jit(solution)/shard_map/reduce_sum | solution.py:99
  172.1 28.5 %all_to_all.18 = f32[16,1,512]{2,1,0:T(1,128)S(1)} all-to-all(f32[16,1,512]{2,1,0:T(1,128)S(1)} %reshape.246), channel_id=1, replica_groups=mesh['date'=16,'strip'=2] {'date'}, dimensions={0} | all-to-all | bytes 65536 | tf_op jit(solution)/shard_map/all_to_all | solution.py:159
  202.5 0.8 copy.169
  203.3 4.7 %reduce_sum.118 = bf16[2,320,320]{2,1,0:T(8,128)(2,1)S(1)} reduce(bf16[16,2,320,320]{3,2,1,0:T(8,128)(2,1)} %bitcast.221, bf16[]{:T(256)} %constant.94.clone.1), dimensions={0}, to_apply=%region_0.1 | reduce | flops 3072000 | bytes 6963202 | tf_op jit(solution)/shard_map/reduce_sum | solution.py:31
  208.0 4.7 %reduce_sum.119 = bf16[2,320,320]{2,1,0:T(8,128)(2,1)S(1)} reduce(bf16[16,2,320,320]{3,2,1,0:T(8,128)(2,1)} %bitcast.222, bf16[]{:T(256)} %constant.94.clone.1), dimensions={0}, to_apply=%region_1.2 | reduce | flops 3072000 | bytes 6963202 | tf_op jit(solution)/shard_map/reduce_sum | solution.py:31
  213.6 0.9 maximum_convert_fusion.1
  215.2 2.8 %slice_bitcast_fusion.3 = (f32[2,5,64,5,64]{4,3,2,1,0:T(8,128)}, f32[2,5,64,5,64]{4,3,2,1,0:T(8,128)}) fusion(f32[2,2,5,64,5,64]{5,4,3,2,1,0:T(8,128)S(1)} %maximum_convert_fusion.1), kind=kLoop, calls=%fused_computation.29 | loop fusion | bytes 3276800 | tf_op jit(solution)/shard_map/mul | solution.py:73
  218.0 2.0 copy.138
  220.0 2.9 %copy.159 = f32[2,5,64,5,64]{2,4,3,1,0:T(8,128)} copy(f32[2,5,64,5,64]{4,3,2,1,0:T(8,128)} %get-tuple-element.21) | data formatting | bytes 1638400 | tf_op jit(solution)/shard_map/mul | solution.py:73
  222.9 4.4 %add_reduce_fusion.1 = (f32[2,2,5,5]{3,2,1,0:T(8,128)S(1)}, f32[2,2,5,5]{3,2,1,0:T(8,128)S(1)}, f32[2,2,5,5]{3,2,1,0:T(8,128)S(1)}) fusion(f32[2,2,2,5,64,5,64]{4,6,2,5,3,1,0:T(8,128)} %get-tuple-element.74, f32[2,5,64,5,64]{2,4,3,1,0:T(8,128)} %copy.159, f32[2,5,64,5,64]{2,4,3,1,0:T(8,128)S(1)} %copy.138), kind=kLoop, calls=%fused_computation.6 | loop fusion | flops 4914900 | bytes 4916400 | tf_op jit(solution)/shard_map/reduce_sum | solution.py:73
  (78 shorter events, 17.4 us)
Async XLA Ops:
  7.2 196.1 %all-gather.5.cloned.1.call-start = ((), (), s32[]{:S(2)}) async-start(), calls=%async_computation.1 | async-start | bytes 8355840 | tf_op jit(solution)/shard_map/all_gather | solution.py:31
  13.2 8.9 %copy-start = (bf16[2,2,2,344,320]{3,4,2,1,0:T(8,128)(2,1)S(1)}, bf16[2,2,2,344,320]{3,4,2,1,0:T(8,128)(2,1)}, u32[]{:S(2)}) copy-start(bf16[2,2,2,344,320]{3,4,2,1,0:T(8,128)(2,1)} %param.5) | copy-start | bytes 5283844
  15.3 13.2 %copy-start.2 = (s32[2,2,2,5,5]{4,2,3,1,0:T(2,128)S(1)}, s32[2,2,2,5,5]{4,2,3,1,0:T(2,128)}, u32[]{:S(2)}) copy-start(s32[2,2,2,5,5]{4,2,3,1,0:T(2,128)} %param.6) | copy-start | bytes 2404
  15.3 13.2 %copy-start.3 = (s32[2,2,2,5,5]{4,2,3,1,0:T(2,128)S(1)}, s32[2,2,2,5,5]{4,2,3,1,0:T(2,128)}, u32[]{:S(2)}) copy-start(s32[2,2,2,5,5]{4,2,3,1,0:T(2,128)} %param.7) | copy-start | bytes 2404
  18.2 189.7 %all-gather.7.cloned.1.call-start = ((), (), s32[]{:S(2)}) async-start(), calls=%async_computation.2 | async-start | bytes 8355840 | tf_op jit(solution)/shard_map/all_gather | solution.py:31
  22.2 13.3 %collective-permute-start.1 = (bf16[2,2,2,344,12]{3,4,2,1,0:T(8,128)(2,1)S(1)}, bf16[2,2,2,344,12]{3,4,2,1,0:T(8,128)(2,1)S(1)}, u32[]{:S(2)}, u32[]{:S(2)}) collective-permute-start(bf16[2,2,2,344,12]{3,4,2,1,0:T(8,128)(2,1)S(1)} %get-tuple-element.24), channel_id=1, source_target_pairs={{1,0},{3,2},{5,4},{7,6},{9,8},{11,10},{13,12},{15,14},{17,16},{19,... | collective-permute-start | bytes 198152 | tf_op jit(solution)/shard_map/ppermute | solution.py:24
  23.5 12.1 %collective-permute-start = (bf16[2,2,2,344,12]{3,4,2,1,0:T(8,128)(2,1)S(1)}, bf16[2,2,2,344,12]{3,4,2,1,0:T(8,128)(2,1)S(1)}, u32[]{:S(2)}, u32[]{:S(2)}) collective-permute-start(bf16[2,2,2,344,12]{3,4,2,1,0:T(8,128)(2,1)S(1)} %get-tuple-element.25), channel_id=1, source_target_pairs={{0,1},{2,3},{4,5},{6,7},{8,9},{10,11},{12,13},{14,15},{16,17},{18,... | collective-permute-start | bytes 198152 | tf_op jit(solution)/shard_map/ppermute | solution.py:21
  88.5 1.7 copy-start.1
  96.5 15.3 %collective-permute-start.2 = (bf16[1,2,2,320,320]{4,3,2,1,0:T(8,128)(2,1)S(1)}, bf16[1,2,2,320,320]{4,3,2,1,0:T(8,128)(2,1)}, u32[]{:S(2)}, u32[]{:S(2)}) collective-permute-start(bf16[1,2,2,320,320]{4,3,2,1,0:T(8,128)(2,1)S(1)} %slice.274), channel_id=1, source_target_pairs={{2,0},{4,2},{6,4},{8,6},{10,8},{12,10},{14,12},{16,14},{18,16},{20... | collective-permute-start | bytes 2457608 | tf_op jit(solution)/shard_map/ppermute | solution.py:37
Sparse Core Ops, SparseCore 0:
  18.4 73.6 all-gather.4
  94.4 76.3 all-gather.6
